TPU v7x, 256 devices: a whole 4x4x8 slice. The times are simulated.
256 devices in a mesh: section: 8 (over y, core), row: 32 (over z, x).
Axes of the slice: x: 4, y: 4, z: 8, core: 2. Of those that a mesh axis runs over, the one named last changes fastest.
Arguments:
- channel_rows_in: bfloat16 [1024, 32, 4096], P('row', None, 'section'), may hold values from -6 to 6
- gate_rows_in: bfloat16 [1024, 32, 4096], P('row', None, 'section'), may hold values from -6 to 6
- map_input_rows: bfloat16 [1024, 32, 256], P('row'), may hold values from -6 to 6
- step_size_input: bfloat16 [1024, 64, 32], P('row', 'section'), may hold values from -4 to 4
- channel_kernel_weight: float32 [4, 4096], P(None, 'section'), may hold values from -3 to 3
- map_kernel_weight: float32 [4, 256], replicated, may hold values from -3 to 3
- channel_conv_bias: float32 [4096], P('section'), may hold values from -3 to 3
- map_kernel_bias: float32 [256], replicated, may hold values from -3 to 3
- step_size_bias: float32 [64], P('section'), may hold values from -2 to 0
- head_decay_rate: float32 [64], P('section'), may hold values from 0.003 to 1
- head_skip_weight: float32 [64], P('section'), may hold values from 0.5 to 1.5
- gated_norm_scale: float32 [4096], P('section'), may hold values from 0.5 to 1.5
- scan_state_cache: bfloat16 [1024, 64, 64, 128], P('row', 'section'), may hold values from -2 to 2
- channel_window_cache: bfloat16 [1024, 3, 4096], P('row', None, 'section'), may hold values from -6 to 6
- map_window_cache: bfloat16 [1024, 3, 256], P('row'), may hold values from -6 to 6
- adapter_down_weight: bfloat16 [32, 64, 4096], P('row', None, 'section'), may hold values from -0.09375 to 0.09375
- adapter_up_weight: bfloat16 [32, 64, 4096], P('row', None, 'section'), may hold values from -0.75 to 0.75
- session_slot_index: int32 [1024], replicated, may hold values from 0 to 1023, as said below
- lengths: int32 [1024], replicated, may hold values from 1 to 32
- session_adapter_index: int32 [1024], replicated, may hold values from 0 to 31
Outputs:
- mixer_output_rows: bfloat16 [1024, 32, 4096], P('row', None, 'section')
- adapter_delta: bfloat16 [1024, 32, 4096], P('row', None, 'section')
- scan_state_next: bfloat16 [1024, 64, 64, 128], P('row', 'section')
- channel_window_next: bfloat16 [1024, 3, 4096], P('row', None, 'section')
- map_window_next: bfloat16 [1024, 3, 256], P('row')
Inputs may be any that keep to these rules, and one draw needn't show every extreme that they name: `session_slot_index`: A permutation of the 1024 cache slots; cache slot c lies on row c // 32 and served session q on row q // 32. The states of one serving row's sessions come from exactly 16 home rows, 2 from each, so every home row also sends to that many rows.
All inputs are finite; a program needn't handle non-finite values.
Results may differ from a plain program's by a relative error of at most 0.0058.
Values may be sent and summed in bfloat16 or wider, within the bound.
No kernel may reach another device: no remote copies, remote signals or barrier semaphores. Data moves between devices by JAX's collectives and lax.ppermute only.
A program may use at most 128 MiB of HBM per device.

v0:
```python
import jax
import jax.numpy as jnp
from jax import lax
from jax.sharding import PartitionSpec as P

INNER_CHANNELS = 4096
NORM_EPS = 1e-05


def sigmoid_linear(value):
    return value / (1.0 + jnp.exp(-value))


def conv_part(cached, fresh, weight, offset):
    extended = jnp.concatenate([cached.astype(jnp.float32), fresh.astype(jnp.float32)], axis=1)
    span_len = fresh.shape[1]
    summed = (
        offset + weight[0] * extended[:, 0:span_len] + weight[1] * extended[:, 1 : span_len + 1]
    )
    summed = (
        summed
        + weight[2] * extended[:, 2 : span_len + 2]
        + weight[3] * extended[:, 3 : span_len + 3]
    )
    return (sigmoid_linear(summed), extended)


def tail_state(extended, lengths):
    total_rows = extended.shape[1]
    picked = lengths[:, None] + jnp.arange(3, dtype=jnp.int32)[None, :]
    onehot = (picked[:, :, None] == jnp.arange(total_rows, dtype=jnp.int32)[None, None, :]).astype(
        jnp.float32
    )
    return jnp.einsum("skt,stc->skc", onehot, extended, precision=lax.Precision.HIGHEST).astype(
        jnp.bfloat16
    )


def mix_sessions(
    channel_rows_in,
    map_input_rows,
    step_size_input,
    lengths,
    scan_state_cache,
    channel_window_cache,
    map_window_cache,
    channel_kernel_weight,
    map_kernel_weight,
    channel_conv_bias,
    map_kernel_bias,
    step_size_bias,
    head_decay_rate,
    head_skip_weight,
):
    highest = lax.Precision.HIGHEST
    local_sess, span_len, channels = channel_rows_in.shape
    head_count = step_size_input.shape[1]
    head_dim = channels // head_count
    state_dim = map_input_rows.shape[2] // 2
    conv_x, ext_x = conv_part(
        channel_window_cache, channel_rows_in, channel_kernel_weight, channel_conv_bias
    )
    conv_m, ext_m = conv_part(map_window_cache, map_input_rows, map_kernel_weight, map_kernel_bias)
    valid = (jnp.arange(span_len, dtype=jnp.int32)[None, :] < lengths[:, None]).astype(jnp.float32)
    step_size = (
        jax.nn.softplus(step_size_input.astype(jnp.float32) + step_size_bias[None, :, None])
        * valid[:, None, :]
    )
    log_decay = jnp.cumsum(-head_decay_rate[None, :, None] * step_size, axis=2)
    input_map = conv_m[:, :, :state_dim]
    output_map = conv_m[:, :, state_dim:]
    x_heads = conv_x.reshape(local_sess, span_len, head_count, head_dim)
    per_block = max(1, 128 // span_len)
    block_count = local_sess // per_block
    block_rows = per_block * span_len
    owners = jnp.arange(block_rows) // span_len
    position = jnp.arange(block_rows)
    causal_mask = (owners[:, None] == owners[None, :]) & (position[:, None] >= position[None, :])
    decay_rows = jnp.transpose(log_decay, (0, 2, 1)).reshape(block_count, block_rows, head_count)
    decay_heads = jnp.transpose(decay_rows, (0, 2, 1))
    spread = decay_heads[:, :, :, None] - decay_heads[:, :, None, :]
    decay_mat = jnp.where(causal_mask, jnp.exp(jnp.where(causal_mask, spread, 0.0)), 0.0)
    in_rows = input_map.reshape(block_count, block_rows, state_dim)
    out_rows = output_map.reshape(block_count, block_rows, state_dim)
    scores = jnp.einsum("btn,bun->btu", out_rows, in_rows, precision=highest)
    step_rows = jnp.transpose(step_size, (0, 2, 1)).reshape(block_count, block_rows, head_count)
    scaled_x = (
        x_heads.reshape(block_count, block_rows, head_count, head_dim) * step_rows[:, :, :, None]
    )
    inside = jnp.einsum("bhtu,buhp->bthp", decay_mat * scores[:, None], scaled_x, precision=highest)
    inside = inside.reshape(local_sess, span_len, head_count, head_dim)
    state_old = scan_state_cache.astype(jnp.float32)
    carried = jnp.einsum("stn,shpn->sthp", output_map, state_old, precision=highest)
    carried = carried * jnp.exp(jnp.transpose(log_decay, (0, 2, 1)))[:, :, :, None]
    mixed_out = (inside + carried + head_skip_weight[None, None, :, None] * x_heads) * valid[
        :, :, None, None
    ]
    final_log = log_decay[:, :, -1]
    weights = jnp.exp(final_log[:, :, None] - log_decay) * step_size
    state_new = jnp.exp(final_log)[:, :, None, None] * state_old
    state_new = state_new + jnp.einsum(
        "sht,sthp,stn->shpn", weights, x_heads, input_map, precision=highest
    )
    return (
        mixed_out.reshape(local_sess, span_len, channels),
        state_new.astype(jnp.bfloat16),
        tail_state(ext_x, lengths),
        tail_state(ext_m, lengths),
    )


def pick_rows(source_rows, take_index, used_mask):
    row_total = source_rows.shape[0]
    onehot = (take_index[:, None] == jnp.arange(row_total, dtype=jnp.int32)[None, :]) & used_mask[
        :, None
    ]
    picked = jnp.dot(
        onehot.astype(source_rows.dtype),
        source_rows,
        preferred_element_type=jnp.float32,
        precision=lax.Precision.HIGHEST,
    )
    return picked.astype(source_rows.dtype)


def select_rows(source_rows, take_index):
    return pick_rows(source_rows, take_index, jnp.ones(take_index.shape, jnp.bool_))


def shards(
    channel_rows_in,
    gate_rows_in,
    map_input_rows,
    step_size_input,
    channel_kernel_weight,
    map_kernel_weight,
    channel_conv_bias,
    map_kernel_bias,
    step_size_bias,
    head_decay_rate,
    head_skip_weight,
    gated_norm_scale,
    scan_state_cache,
    channel_window_cache,
    map_window_cache,
    adapter_down_weight,
    adapter_up_weight,
    session_slot_index,
    lengths,
    session_adapter_index,
):
    local_sess = channel_rows_in.shape[0]
    row_count = lax.axis_size("row")
    row_index = lax.axis_index("row")
    capacity = max(2, 2 * local_sess // row_count)
    slot_count = row_count * capacity
    home_rows = (session_slot_index // local_sess).reshape(row_count, local_sess)
    same_home = home_rows[:, :, None] == home_rows[:, None, :]
    earlier = jnp.arange(local_sess)[None, :] < jnp.arange(local_sess)[:, None]
    rank_in_pair = (
        jnp.sum(jnp.where(same_home & earlier[None], 1, 0), axis=2).astype(jnp.int32).reshape(-1)
    )
    serve_rows = jnp.arange(row_count * local_sess, dtype=jnp.int32) // local_sess
    target = serve_rows * capacity + rank_in_pair
    source = session_slot_index // local_sess * capacity + rank_in_pair
    serve_slots = lax.dynamic_slice_in_dim(source, row_index * local_sess, local_sess)
    serve_lengths = lax.dynamic_slice_in_dim(lengths, row_index * local_sess, local_sess)
    serve_adapter = lax.dynamic_slice_in_dim(
        session_adapter_index, row_index * local_sess, local_sess
    )
    local_cache = jnp.arange(local_sess, dtype=jnp.int32) + row_index * local_sess
    cache_match = session_slot_index[None, :] == local_cache[:, None]
    home_slots = jnp.sum(jnp.where(cache_match, target[None, :], 0), axis=1)
    slot_range = jnp.arange(slot_count, dtype=jnp.int32)[:, None]
    local_range = jnp.arange(local_sess, dtype=jnp.int32)[None, :]
    home_fill = slot_range == home_slots[None, :]
    home_take = jnp.sum(jnp.where(home_fill, local_range, 0), axis=1)
    home_used = jnp.any(home_fill, axis=1)
    serve_fill = slot_range == serve_slots[None, :]
    serve_take = jnp.sum(jnp.where(serve_fill, local_range, 0), axis=1)
    serve_used = jnp.any(serve_fill, axis=1)
    layer_params = (
        channel_kernel_weight,
        map_kernel_weight,
        channel_conv_bias,
        map_kernel_bias,
        step_size_bias,
        head_decay_rate,
        head_skip_weight,
    )
    received = (
        lax.all_to_all(
            pick_rows(scan_state_cache.reshape(local_sess, -1), home_take, home_used),
            "row",
            split_axis=0,
            concat_axis=0,
            tiled=True,
        ),
        lax.all_to_all(
            pick_rows(channel_window_cache.reshape(local_sess, -1), home_take, home_used),
            "row",
            split_axis=0,
            concat_axis=0,
            tiled=True,
        ),
        lax.all_to_all(
            pick_rows(map_window_cache.reshape(local_sess, -1), home_take, home_used),
            "row",
            split_axis=0,
            concat_axis=0,
            tiled=True,
        ),
    )
    state_here = select_rows(received[0], serve_slots).reshape(scan_state_cache.shape)
    conv_here = select_rows(received[1], serve_slots).reshape(channel_window_cache.shape)
    map_here = select_rows(received[2], serve_slots).reshape(map_window_cache.shape)
    mixed, state_new, conv_new, map_new = mix_sessions(
        channel_rows_in,
        map_input_rows,
        step_size_input,
        serve_lengths,
        state_here,
        conv_here,
        map_here,
        *layer_params
    )
    returned = (
        lax.all_to_all(
            pick_rows(state_new.reshape(local_sess, -1), serve_take, serve_used),
            "row",
            split_axis=0,
            concat_axis=0,
            tiled=True,
        ),
        lax.all_to_all(
            pick_rows(conv_new.reshape(local_sess, -1), serve_take, serve_used),
            "row",
            split_axis=0,
            concat_axis=0,
            tiled=True,
        ),
        lax.all_to_all(
            pick_rows(map_new.reshape(local_sess, -1), serve_take, serve_used),
            "row",
            split_axis=0,
            concat_axis=0,
            tiled=True,
        ),
    )
    scan_state_next = select_rows(returned[0], home_slots).reshape(scan_state_cache.shape)
    channel_window_next = select_rows(returned[1], home_slots).reshape(channel_window_cache.shape)
    map_window_next = select_rows(returned[2], home_slots).reshape(map_window_cache.shape)
    gated = mixed * sigmoid_linear(gate_rows_in.astype(jnp.float32))
    square_sum = lax.psum(jnp.sum(gated * gated, axis=2), "section")
    inv_rms = lax.rsqrt(square_sum / INNER_CHANNELS + NORM_EPS)
    mixer_output_rows = (gated * inv_rms[:, :, None] * gated_norm_scale).astype(jnp.bfloat16)
    pieces = (
        lax.all_gather(adapter_down_weight, "row", axis=0, tiled=True),
        lax.all_gather(adapter_up_weight, "row", axis=0, tiled=True),
    )
    piece_len = pieces[0].shape[0]
    chosen = (serve_adapter[:, None] == jnp.arange(piece_len, dtype=jnp.int32)[None, :]).astype(
        jnp.bfloat16
    )
    down_part = jnp.einsum("sk,krc->src", chosen, pieces[0], preferred_element_type=jnp.float32)
    up_part = jnp.einsum("sk,krc->src", chosen, pieces[1], preferred_element_type=jnp.float32)
    low_part = jnp.einsum(
        "std,srd->str",
        mixer_output_rows,
        down_part.astype(jnp.bfloat16),
        preferred_element_type=jnp.float32,
    )
    low_total = lax.psum(low_part, "section").astype(jnp.bfloat16)
    adapter_delta = jnp.einsum(
        "str,src->stc", low_total, up_part.astype(jnp.bfloat16), preferred_element_type=jnp.float32
    ).astype(jnp.bfloat16)
    return (mixer_output_rows, adapter_delta, scan_state_next, channel_window_next, map_window_next)


def solution(mesh):
    return jax.shard_map(
        shards,
        mesh=mesh,
        in_specs=(
            P("row", None, "section"),
            P("row", None, "section"),
            P("row", None, None),
            P("row", "section", None),
            P(None, "section"),
            P(),
            P("section"),
            P(),
            P("section"),
            P("section"),
            P("section"),
            P("section"),
            P("row", "section", None, None),
            P("row", None, "section"),
            P("row", None, None),
            P("row", None, "section"),
            P("row", None, "section"),
            P(),
            P(),
            P(),
        ),
        out_specs=(
            P("row", None, "section"),
            P("row", None, "section"),
            P("row", "section", None, None),
            P("row", None, "section"),
            P("row", None, None),
        ),
        check_vma=False,
    )
```

profile of v0, /device:TPU:6, one launch (start us, length us, event | category | flops | bytes accessed | tf_op | source)
XLA Modules:
  0.0 662.8 jit_solution(1876397155071708182)
XLA Ops:
  12.7 11.6 %all-to-all-start.1 = ((bf16[32,2,768]{2,1,0:T(2,128)(2,1)}), bf16[32,2,768]{2,1,0:T(2,128)(2,1)S(1)}, u32[]{:S(2)}, u32[]{:S(2)}) async-start(bf16[32,2,768]{2,1,0:T(2,128)(2,1)} %all_to_all.51), calls=%async_computation.1 | async-start | bytes 196608 | tf_op jit(solution)/shard_map/all_to_all | solution.py:206
  26.2 6.7 %all-to-all-done.1 = bf16[32,2,768]{2,1,0:T(2,128)(2,1)S(1)} async-done(((bf16[32,2,768]{2,1,0:T(2,128)(2,1)}), bf16[32,2,768]{2,1,0:T(2,128)(2,1)S(1)}, u32[]{:S(2)}, u32[]{:S(2)}) %all-to-all-start.1) | async-done | bytes 98336 | tf_op jit(solution)/shard_map/all_to_all | solution.py:206
  32.9 5.4 all-to-all-start
  38.3 8.3 %convolution_convert_fusion.1 = bf16[64,65536]{1,0:T(8,128)(2,1)} fusion(bf16[4,8,512,128]{3,2,1,0:T(8,128)(2,1)} %bitcast.95, s32[64]{0:T(128)S(1)} %select_reduce_fusion.3, pred[64]{0:T(512)(128)(4,1)S(1)} %fusion.97), kind=kOutput, calls=%fused_computation.1 | convolution fusion | flops 272633856 | bytes 12583232 | tf_op jit(solution)/shard_map/dot_general | solution.py:117
  46.6 10.5 %all_to_all.54 = bf16[32,2,65536]{2,1,0:T(2,128)(2,1)} reshape(bf16[64,65536]{1,0:T(8,128)(2,1)} %convolution_convert_fusion.1) | data formatting | bytes 16777216 | tf_op jit(solution)/shard_map/all_to_all | solution.py:192
  57.1 10.4 %all-to-all-start.2 = ((bf16[32,2,65536]{2,1,0:T(2,128)(2,1)}), bf16[32,2,65536]{2,1,0:T(2,128)(2,1)}, u32[]{:S(2)}, u32[]{:S(2)}) async-start(bf16[32,2,65536]{2,1,0:T(2,128)(2,1)} %all_to_all.54), calls=%async_computation.2 | async-start | bytes 16777216 | tf_op jit(solution)/shard_map/all_to_all | solution.py:192
  68.7 5.9 reduce_window_sum.11
  83.5 4.7 add_divide_fusion
  95.1 4.3 broadcast_multiply_fusion
  99.4 153.6 %all-to-all-done.2 = bf16[32,2,65536]{2,1,0:T(2,128)(2,1)} async-done(((bf16[32,2,65536]{2,1,0:T(2,128)(2,1)}), bf16[32,2,65536]{2,1,0:T(2,128)(2,1)}, u32[]{:S(2)}, u32[]{:S(2)}) %all-to-all-start.2) | async-done | bytes 8388640 | tf_op jit(solution)/shard_map/all_to_all | solution.py:192
  253.0 9.6 %all-to-all-start.5 = ((bf16[32,2,768]{2,1,0:T(2,128)(2,1)}), bf16[32,2,768]{2,1,0:T(2,128)(2,1)S(1)}, u32[]{:S(2)}, u32[]{:S(2)}) async-start(bf16[32,2,768]{2,1,0:T(2,128)(2,1)} %all_to_all.63), calls=%async_computation.5 | async-start | bytes 196608 | tf_op jit(solution)/shard_map/all_to_all | solution.py:242
  262.6 10.2 %all_to_all.56 = bf16[64,65536]{1,0:T(8,128)(2,1)} reshape(bf16[32,2,65536]{2,1,0:T(2,128)(2,1)} %all-to-all-done.2) | data formatting | bytes 16777216 | tf_op jit(solution)/shard_map/all_to_all | solution.py:192
  272.8 4.7 fusion.19
  280.5 15.8 %add_convert_fusion = bf16[32,8,64,128]{3,2,1,0:T(8,128)(2,1)} fusion(bf16[32,8,64,128]{3,2,1,0:T(8,128)(2,1)S(1)} %bitcast.91, f32[32,8]{1,0:T(8,128)S(1)} %copy-done.15, f32[32,32,8,64]{3,2,1,0:T(8,128)S(1)} %copy-done.2, f32[32,32,256]{2,1,0:T(8,128)S(1)} %add_divide_fusion.1), kind=kOutput, calls=%fused_computation.4 | convolution fusion | flops 813694976 | bytes 13123584 | tf_op jit(solution)/shard_map/sht,sthp,stn->shpn/dot_general | solution.py:101
  296.9 9.8 %all-to-all-start.4 = ((bf16[32,2,1536]{2,1,0:T(2,128)(2,1)}), bf16[32,2,1536]{2,1,0:T(2,128)(2,1)S(1)}, u32[]{:S(2)}, u32[]{:S(2)}) async-start(bf16[32,2,1536]{2,1,0:T(2,128)(2,1)} %all_to_all.60), calls=%async_computation.4 | async-start | bytes 393216 | tf_op jit(solution)/shard_map/all_to_all | solution.py:235
  306.7 8.3 %convolution_convert_fusion = bf16[64,65536]{1,0:T(8,128)(2,1)} fusion(bf16[4,8,512,128]{3,2,1,0:T(8,128)(2,1)} %bitcast.93, s32[64]{0:T(128)S(1)} %copy-done.20, pred[64]{0:T(512)(128)(4,1)S(1)} %copy-done.22), kind=kOutput, calls=%fused_computation | convolution fusion | flops 272633856 | bytes 12583232 | tf_op jit(solution)/shard_map/dot_general | solution.py:117
  315.0 10.5 %all_to_all.57 = bf16[32,2,65536]{2,1,0:T(2,128)(2,1)} reshape(bf16[64,65536]{1,0:T(8,128)(2,1)} %convolution_convert_fusion) | data formatting | bytes 16777216 | tf_op jit(solution)/shard_map/all_to_all | solution.py:228
  325.6 9.8 %all-to-all-start.3 = ((bf16[32,2,65536]{2,1,0:T(2,128)(2,1)}), bf16[32,2,65536]{2,1,0:T(2,128)(2,1)}, u32[]{:S(2)}, u32[]{:S(2)}) async-start(bf16[32,2,65536]{2,1,0:T(2,128)(2,1)} %all_to_all.57), calls=%async_computation.3 | async-start | bytes 16777216 | tf_op jit(solution)/shard_map/all_to_all | solution.py:228
  347.2 3.7 broadcast_multiply_fusion.1
  350.9 8.9 %fusion.53 = f32[8,128,8,64]{1,3,2,0:T(8,128)S(1)} fusion(f32[8,128,128]{2,1,0:T(8,128)S(1)} %copy-done.10, f32[8,8,128]{2,1,0:T(8,128)S(1)} %copy.74, pred[128,128]{1,0:T(8,128)(4,1)S(1)} %fusion.79, f32[8,128,8,64]{3,2,1,0:T(8,128)S(1)} %broadcast_multiply_fusion.1), kind=kOutput, calls=%fused_computation.76 | convolution fusion | flops 809500672 | bytes 4767744 | tf_op jit(solution)/shard_map/bhtu,buhp->bthp/dot_general | solution.py:90
  364.6 87.1 %all-gather.5.cloned.1.call-done = bf16[32,64,512]{2,1,0:T(8,128)(2,1)} async-done(((bf16[1,64,512]{2,1,0:T(8,128)(2,1)}), bf16[32,64,512]{2,1,0:T(8,128)(2,1)}) %all-gather.5.cloned.1.call-update) | async-done | bytes 2097168 | tf_op jit(solution)/shard_map/all_gather | solution.py:259
  451.7 4.6 fusion.50
  456.3 92.9 %all-gather.3.cloned.1.call-done = bf16[32,64,512]{2,1,0:T(8,128)(2,1)} async-done(((bf16[1,64,512]{2,1,0:T(8,128)(2,1)}), bf16[32,64,512]{2,1,0:T(8,128)(2,1)}) %all-gather.3.cloned.1.call-update) | async-done | bytes 2097168 | tf_op jit(solution)/shard_map/all_gather | solution.py:258
  549.2 4.8 fusion.47
  553.9 13.9 %fusion.7 = f32[32,32,8,64]{3,1,2,0:T(8,128)S(1)} fusion(f32[32,32,8,64]{3,2,1,0:T(8,128)S(1)} %copy-done, f32[32,32,8,64]{3,2,1,0:T(8,128)} %bitcast.94, bf16[32,8,64,128]{3,2,1,0:T(8,128)(2,1)} %bitcast.92, f32[32,32]{1,0:T(8,128)S(1)} %fusion.104, f32[8]{0:T(128)S(1)} %copy-done.30, f32[32,32,8]{1,2,0:T(8,128)S(1)} %copy-done.8, ...), kind=kOutput, calls=%fused_computation.17 | convolution fusion | flops 807927808 | bytes 13255168 | tf_op jit(solution)/shard_map/stn,shpn->sthp/dot_general | solution.py:93
  567.9 5.8 copy.81
  573.7 3.5 reshape.245
  578.0 24.2 %psum.14 = f32[32,32]{1,0:T(8,128)S(1)} all-reduce(f32[32,32]{1,0:T(8,128)S(1)} %multiply_reduce_fusion), channel_id=1, replica_groups=mesh['section'=8,'row'=32] {'section'}, use_global_device_ids=true, to_apply=%region_6.7 | all-reduce | flops 1024 | bytes 8192 | tf_op jit(solution)/shard_map/psum | solution.py:254
  605.2 29.2 %all-reduce.1 = bf16[32,32,64]{2,1,0:T(8,128)(2,1)S(1)} all-reduce(f32[32,32,64]{2,1,0:T(8,128)S(1)} %fusion.38), channel_id=1, replica_groups=mesh['section'=8,'row'=32] {'section'}, use_global_device_ids=true, to_apply=%region_7.8 | all-reduce | flops 65536 | bytes 393216 | tf_op jit(solution)/shard_map/psum | solution.py:273
  634.3 3.6 fusion.58
  637.9 10.2 %all_to_all.59 = bf16[64,65536]{1,0:T(8,128)(2,1)} reshape(bf16[32,2,65536]{2,1,0:T(2,128)(2,1)} %all-to-all-done.3) | data formatting | bytes 16777216 | tf_op jit(solution)/shard_map/all_to_all | solution.py:228
  648.1 4.7 fusion.20
  (147 shorter events, 50.9 us)
Async XLA Ops:
  12.7 20.2 %all-to-all-start.1 = ((bf16[32,2,768]{2,1,0:T(2,128)(2,1)}), bf16[32,2,768]{2,1,0:T(2,128)(2,1)S(1)}, u32[]{:S(2)}, u32[]{:S(2)}) async-start(bf16[32,2,768]{2,1,0:T(2,128)(2,1)} %all_to_all.51), calls=%async_computation.1 | async-start | bytes 196608 | tf_op jit(solution)/shard_map/all_to_all | solution.py:206
  32.9 24.2 %all-to-all-start = ((bf16[32,2,1536]{2,1,0:T(2,128)(2,1)}), bf16[32,2,1536]{2,1,0:T(2,128)(2,1)S(1)}, u32[]{:S(2)}, u32[]{:S(2)}) async-start(bf16[32,2,1536]{2,1,0:T(2,128)(2,1)} %all_to_all.48), calls=%async_computation | async-start | bytes 393216 | tf_op jit(solution)/shard_map/all_to_all | solution.py:199
  57.1 10.5 %copy-start.31 = (f32[8]{0:T(128)S(1)}, f32[8]{0:T(128)}, u32[]{:S(2)}) copy-start(f32[8]{0:T(128)} %param.29) | copy-start | bytes 100
  57.1 11.4 %copy-start.13 = (bf16[32,8,32]{2,1,0:T(8,128)(2,1)S(1)}, bf16[32,8,32]{2,1,0:T(8,128)(2,1)}, u32[]{:S(2)}) copy-start(bf16[32,8,32]{2,1,0:T(8,128)(2,1)} %param.23) | copy-start | bytes 49156
  57.1 11.4 %copy-start.27 = (f32[8]{0:T(128)S(1)}, f32[8]{0:T(128)}, u32[]{:S(2)}) copy-start(f32[8]{0:T(128)} %param.28) | copy-start | bytes 100
  57.1 18.0 %copy-start.7 = (bf16[32,32,512]{2,1,0:T(8,128)(2,1)S(1)}, bf16[32,32,512]{2,1,0:T(8,128)(2,1)}, u32[]{:S(2)}) copy-start(bf16[32,32,512]{2,1,0:T(8,128)(2,1)} %param.20) | copy-start | bytes 3145732
  57.1 195.9 %all-to-all-start.2 = ((bf16[32,2,65536]{2,1,0:T(2,128)(2,1)}), bf16[32,2,65536]{2,1,0:T(2,128)(2,1)}, u32[]{:S(2)}, u32[]{:S(2)}) async-start(bf16[32,2,65536]{2,1,0:T(2,128)(2,1)} %all_to_all.54), calls=%async_computation.2 | async-start | bytes 16777216 | tf_op jit(solution)/shard_map/all_to_all | solution.py:192
  67.6 9.2 %copy-start.9 = (bf16[32,32,256]{2,1,0:T(8,128)(2,1)S(1)}, bf16[32,32,256]{2,1,0:T(8,128)(2,1)}, u32[]{:S(2)}) copy-start(bf16[32,32,256]{2,1,0:T(8,128)(2,1)} %param.22) | copy-start | bytes 1572868
  67.6 12.1 %copy-start.25 = (f32[4,256]{1,0:T(4,128)S(1)}, f32[4,256]{1,0:T(4,128)}, u32[]{:S(2)}) copy-start(f32[4,256]{1,0:T(4,128)} %param.25) | copy-start | bytes 12292
  67.6 12.1 %copy-start.18 = (f32[4,512]{1,0:T(4,128)S(1)}, f32[4,512]{1,0:T(4,128)}, u32[]{:S(2)}) copy-start(f32[4,512]{1,0:T(4,128)} %param.24) | copy-start | bytes 24580
  74.9 7.3 %copy-start.29 = (f32[256]{0:T(256)S(1)}, f32[256]{0:T(256)}, u32[]{:S(2)}) copy-start(f32[256]{0:T(256)} %param.27) | copy-start | bytes 3076
  76.8 6.7 %copy-start.23 = (s32[32]{0:T(128)}, s32[32]{0:T(128)S(1)}, u32[]{:S(2)}) copy-start(s32[32]{0:T(128)S(1)} %dynamic_slice.9) | copy-start | bytes 388
  79.6 3.5 copy-start.19
  79.7 3.4 copy-start.21
  253.0 43.3 %all-to-all-start.5 = ((bf16[32,2,768]{2,1,0:T(2,128)(2,1)}), bf16[32,2,768]{2,1,0:T(2,128)(2,1)S(1)}, u32[]{:S(2)}, u32[]{:S(2)}) async-start(bf16[32,2,768]{2,1,0:T(2,128)(2,1)} %all_to_all.63), calls=%async_computation.5 | async-start | bytes 196608 | tf_op jit(solution)/shard_map/all_to_all | solution.py:242
  262.6 10.2 %copy-start.24 = (s32[32]{0:T(128)S(1)}, s32[32]{0:T(128)}, u32[]{:S(2)}) copy-start(s32[32]{0:T(128)} %copy-done.23) | copy-start | bytes 388
  280.4 26.3 %copy-start.20 = (s32[64]{0:T(128)S(1)}, s32[64]{0:T(128)}, u32[]{:S(2)}) copy-start(s32[64]{0:T(128)} %copy-done.19) | copy-start | bytes 772
  280.4 26.3 %copy-start.22 = (pred[64]{0:T(512)(128)(4,1)S(1)}, pred[64]{0:T(512)(128)(4,1)}, u32[]{:S(2)}) copy-start(pred[64]{0:T(512)(128)(4,1)} %copy-done.21) | copy-start | bytes 196
  296.9 28.7 %all-to-all-start.4 = ((bf16[32,2,1536]{2,1,0:T(2,128)(2,1)}), bf16[32,2,1536]{2,1,0:T(2,128)(2,1)S(1)}, u32[]{:S(2)}, u32[]{:S(2)}) async-start(bf16[32,2,1536]{2,1,0:T(2,128)(2,1)} %all_to_all.60), calls=%async_computation.4 | async-start | bytes 393216 | tf_op jit(solution)/shard_map/all_to_all | solution.py:235
  325.6 312.3 %all-to-all-start.3 = ((bf16[32,2,65536]{2,1,0:T(2,128)(2,1)}), bf16[32,2,65536]{2,1,0:T(2,128)(2,1)}, u32[]{:S(2)}, u32[]{:S(2)}) async-start(bf16[32,2,65536]{2,1,0:T(2,128)(2,1)} %all_to_all.57), calls=%async_computation.3 | async-start | bytes 16777216 | tf_op jit(solution)/shard_map/all_to_all | solution.py:228
  335.4 116.3 %all-gather.5.cloned.1.call-start = ((), (), s32[]{:S(2)}) async-start(), calls=%async_computation.7 | async-start | bytes 2162688 | tf_op jit(solution)/shard_map/all_gather | solution.py:259
  336.2 213.0 %all-gather.3.cloned.1.call-start = ((), (), s32[]{:S(2)}) async-start(), calls=%async_computation.6 | async-start | bytes 2162688 | tf_op jit(solution)/shard_map/all_gather | solution.py:258
  347.2 3.7 copy-start.10
  359.8 3.0 copy-start.12
  359.8 3.0 copy-start.17
  359.8 91.9 %copy-start.28 = (s32[32]{0:T(128)S(1)}, s32[32]{0:T(128)}, u32[]{:S(2)}) copy-start(s32[32]{0:T(128)} %dynamic_slice.11) | copy-start | bytes 388
  364.6 189.4 %copy-start.8 = (f32[32,32,8]{1,2,0:T(8,128)S(1)}, f32[32,32,8]{1,2,0:T(8,128)}, u32[]{:S(2)}) copy-start(f32[32,32,8]{1,2,0:T(8,128)} %bitcast_exponential_fusion.1) | copy-start | bytes 98308
  364.6 189.4 %copy-start.30 = (f32[8]{0:T(128)S(1)}, f32[8]{0:T(128)}, u32[]{:S(2)}) copy-start(f32[8]{0:T(128)} %param.30) | copy-start | bytes 100
  549.2 4.8 copy-start
  573.7 3.5 copy-start.5
  573.7 28.5 %copy-start.26 = (f32[512]{0:T(512)S(1)}, f32[512]{0:T(512)}, u32[]{:S(2)}) copy-start(f32[512]{0:T(512)} %param.31) | copy-start | bytes 6148
  603.9 30.4 %copy-start.4 = (bf16[32,64,512]{2,0,1:T(8,128)(2,1)S(1)}, bf16[32,64,512]{2,0,1:T(8,128)(2,1)}, u32[]{:S(2)}) copy-start(bf16[32,64,512]{2,0,1:T(8,128)(2,1)} %fusion.50) | copy-start | bytes 6291460
  (8 other events, 12.7 us)
Sparse Core Ops, SparseCore 0:
  338.8 112.8 all-gather.4
  454.2 94.8 all-gather.2
where the time goes:
time: 669 us; the launch traced here: 663 us
  waiting for transfers between devices  341 us (51%)
  matrix products  86.7 us (13%)
  local copies, waits for them, and re-layouts  82.4 us (12%)
  starting transfers between devices  57.1 us (9%)
  blocking collectives  53.3 us (8%)
  other arithmetic  27.2 us (4%)
  between operations  14.8 us (2%)
    all_to_all x1, waiting for transfers between devices, shards(): lax.all_to_all(pick_rows(scan_state_cache.reshape(local_sess, -1), home_t...  154 us
    all_gather x1, waiting for transfers between devices, shards(): lax.all_gather(adapter_down_weight, 'row', axis=0, tiled=True)  92.9 us
    all_gather x1, waiting for transfers between devices, shards(): lax.all_gather(adapter_up_weight, 'row', axis=0, tiled=True)  87.1 us
    psum x1, blocking collectives, shards(): low_total = lax.psum(low_part, 'section').astype(jnp.bfloat16)  29.2 us
    dot_general x12, matrix products, pick_rows(): jnp.dot(onehot.astype(source_rows.dtype), source_rows, preferred_element_...  28.4 us
    psum x1, blocking collectives, shards(): square_sum = lax.psum(jnp.sum(gated * gated, axis=2), 'section')  24.2 us
    all_to_all x2, local copies, waits for them, and re-layouts, shards(): lax.all_to_all(pick_rows(scan_state_cache.reshape(local_sess, -1), home_t...  20.7 us
    all_to_all x2, local copies, waits for them, and re-layouts, shards(): lax.all_to_all(pick_rows(state_new.reshape(local_sess, -1), serve_take, s...  20.7 us
  transfers between devices with their start and end apart: 8, of which 4 were waited for; matrix products, arithmetic and copies ran while one was open for 20% of the time, Pallas kernels for 0%

commit v1 on v0

--- a/solution.py
+++ b/solution.py
@@ -149,6 +149,12 @@
     lengths,
     session_adapter_index,
 ):
+
+    def prepare_ends_now(local_block, chip_axis, on_dim):
+        plain = jnp.stack([local_block for _ in range(lax.psum(1, chip_axis))])
+        arr_next = lax.all_to_all(plain, chip_axis, 0, 0)
+        return jnp.concatenate(arr_next, on_dim)
+
     local_sess = channel_rows_in.shape[0]
     row_count = lax.axis_size("row")
     row_index = lax.axis_index("row")
@@ -256,7 +262,7 @@
     mixer_output_rows = (gated * inv_rms[:, :, None] * gated_norm_scale).astype(jnp.bfloat16)
     pieces = (
         lax.all_gather(adapter_down_weight, "row", axis=0, tiled=True),
-        lax.all_gather(adapter_up_weight, "row", axis=0, tiled=True),
+        prepare_ends_now(adapter_up_weight, "row", 0),
     )
     piece_len = pieces[0].shape[0]
     chosen = (serve_adapter[:, None] == jnp.arange(piece_len, dtype=jnp.int32)[None, :]).astype(

time: 669 us -> 645 us (0.964)
  waiting for transfers between devices: 341 us -> 298 us
    all_gather x1 -> x0, waiting for transfers between devices: 87.1 us -> none  [shards(): lax.all_gather(adapter_up_weight, 'row', axis=0, tiled=True)]
    all_to_all x1, waiting for transfers between devices: 154 us -> 180 us  [shards(): lax.all_to_all(pick_rows(scan_state_cache.reshape(local_sess, -1), home_t...]
    all_gather x1, waiting for transfers between devices: 92.9 us -> 109 us  [shards(): lax.all_gather(adapter_down_weight, 'row', axis=0, tiled=True)]
    all_to_all x0 -> x1, starting transfers between devices: none -> 9.76 us  [prepare_ends_now(): arr_next = lax.all_to_all(plain, chip_axis, 0, 0)]
  transfers between devices with their start and end apart: 8 -> 8, of which waited for: 4 -> 5; matrix products, arithmetic and copies ran while one was open for 20% -> 21% of each run, Pallas kernels for 0% -> 0%
where the time goes in v1:
time: 645 us; the launch traced here: 634 us
  waiting for transfers between devices  298 us (46%)
  local copies, waits for them, and re-layouts  87.4 us (14%)
  matrix products  85.3 us (13%)
  starting transfers between devices  62.7 us (10%)
  blocking collectives  56.6 us (9%)
  other arithmetic  29 us (4%)
  between operations  15.1 us (2%)
    all_to_all x1, waiting for transfers between devices, shards(): lax.all_to_all(pick_rows(scan_state_cache.reshape(local_sess, -1), home_t...  180 us
    all_gather x1, waiting for transfers between devices, shards(): lax.all_gather(adapter_down_weight, 'row', axis=0, tiled=True)  109 us
    dot_general x12, matrix products, pick_rows(): jnp.dot(onehot.astype(source_rows.dtype), source_rows, preferred_element_...  29.9 us
    psum x1, blocking collectives, shards(): low_total = lax.psum(low_part, 'section').astype(jnp.bfloat16)  29.2 us
    psum x1, blocking collectives, shards(): square_sum = lax.psum(jnp.sum(gated * gated, axis=2), 'section')  27.4 us
    all_to_all x2, local copies, waits for them, and re-layouts, shards(): lax.all_to_all(pick_rows(state_new.reshape(local_sess, -1), serve_take, s...  20.9 us
    all_to_all x2, local copies, waits for them, and re-layouts, shards(): lax.all_to_all(pick_rows(scan_state_cache.reshape(local_sess, -1), home_t...  20.8 us
    dot_general x1, matrix products, mix_sessions(): jnp.einsum('sht,sthp,stn->shpn', weights, x_heads, input_map, precision=h...  14.5 us
  transfers between devices with their start and end apart: 8, of which 5 were waited for; matrix products, arithmetic and copies ran while one was open for 21% of the time, Pallas kernels for 0%

profile of v1, /device:TPU:6, one launch (start us, length us, event | category | flops | bytes accessed | tf_op | source)
XLA Modules:
  0.0 634.1 jit_solution(7812461579881111198)
XLA Ops:
  12.7 11.6 %all-to-all-start.1 = ((bf16[32,2,768]{2,1,0:T(2,128)(2,1)}), bf16[32,2,768]{2,1,0:T(2,128)(2,1)S(1)}, u32[]{:S(2)}, u32[]{:S(2)}) async-start(bf16[32,2,768]{2,1,0:T(2,128)(2,1)} %all_to_all.54), calls=%async_computation.1 | async-start | bytes 196608 | tf_op jit(solution)/shard_map/all_to_all | solution.py:212
  32.9 6.9 %all-to-all-start = ((bf16[32,2,1536]{2,1,0:T(2,128)(2,1)}), bf16[32,2,1536]{2,1,0:T(2,128)(2,1)S(1)}, u32[]{:S(2)}, u32[]{:S(2)}) async-start(bf16[32,2,1536]{2,1,0:T(2,128)(2,1)} %all_to_all.51), calls=%async_computation | async-start | bytes 393216 | tf_op jit(solution)/shard_map/all_to_all | solution.py:205
  46.4 3.1 all-to-all-done
  49.4 6.8 %all-to-all-start.6 = ((bf16[32,2,768]{2,1,0:T(2,128)(2,1)}), bf16[32,2,768]{2,1,0:T(2,128)(2,1)}, u32[]{:S(2)}, u32[]{:S(2)}) async-start(bf16[32,2,768]{2,1,0:T(2,128)(2,1)} %all_to_all.67), calls=%async_computation.6 | async-start | bytes 196608 | tf_op jit(solution)/shard_map/all_to_all | solution.py:248
  64.9 7.6 %all-to-all-start.5 = ((bf16[32,2,1536]{2,1,0:T(2,128)(2,1)}), bf16[32,2,1536]{2,1,0:T(2,128)(2,1)S(1)}, u32[]{:S(2)}, u32[]{:S(2)}) async-start(bf16[32,2,1536]{2,1,0:T(2,128)(2,1)} %all_to_all.64), calls=%async_computation.5 | async-start | bytes 393216 | tf_op jit(solution)/shard_map/all_to_all | solution.py:241
  72.5 8.3 %convolution_convert_fusion.1 = bf16[64,65536]{1,0:T(8,128)(2,1)} fusion(bf16[4,8,512,128]{3,2,1,0:T(8,128)(2,1)} %bitcast.101, s32[64]{0:T(128)} %copy-done.28, pred[64]{0:T(512)(128)(4,1)} %copy-done.29), kind=kOutput, calls=%fused_computation.1 | convolution fusion | flops 272633856 | bytes 12583232 | tf_op jit(solution)/shard_map/dot_general | solution.py:117
  80.8 10.5 %all_to_all.57 = bf16[32,2,65536]{2,1,0:T(2,128)(2,1)} reshape(bf16[64,65536]{1,0:T(8,128)(2,1)} %convolution_convert_fusion.1) | data formatting | bytes 16777216 | tf_op jit(solution)/shard_map/all_to_all | solution.py:198
  92.1 9.8 %all-to-all-start.2 = ((bf16[32,2,65536]{2,1,0:T(2,128)(2,1)}), bf16[32,2,65536]{2,1,0:T(2,128)(2,1)}, u32[]{:S(2)}, u32[]{:S(2)}) async-start(bf16[32,2,65536]{2,1,0:T(2,128)(2,1)} %all_to_all.57), calls=%async_computation.2 | async-start | bytes 16777216 | tf_op jit(solution)/shard_map/all_to_all | solution.py:198
  102.1 180.3 %all-to-all-done.2 = bf16[32,2,65536]{2,1,0:T(2,128)(2,1)} async-done(((bf16[32,2,65536]{2,1,0:T(2,128)(2,1)}), bf16[32,2,65536]{2,1,0:T(2,128)(2,1)}, u32[]{:S(2)}, u32[]{:S(2)}) %all-to-all-start.2) | async-done | bytes 8388640 | tf_op jit(solution)/shard_map/all_to_all | solution.py:198
  284.0 9.8 %all-to-all-start.3 = ((bf16[32,1,64,512]{3,2,1,0:T(8,128)(2,1)}), bf16[32,1,64,512]{3,2,1,0:T(8,128)(2,1)}, u32[]{:S(2)}, u32[]{:S(2)}) async-start(bf16[32,1,64,512]{3,2,1,0:T(8,128)(2,1)} %stack.2), calls=%async_computation.3 | async-start | bytes 4194304 | tf_op jit(solution)/shard_map/all_to_all | solution.py:155
  293.9 5.9 reduce_window_sum.11
  304.6 4.6 add_divide_fusion
  311.7 4.2 broadcast_multiply_fusion
  316.0 10.2 %all_to_all.59 = bf16[64,65536]{1,0:T(8,128)(2,1)} reshape(bf16[32,2,65536]{2,1,0:T(2,128)(2,1)} %all-to-all-done.2) | data formatting | bytes 16777216 | tf_op jit(solution)/shard_map/all_to_all | solution.py:198
  326.2 4.7 fusion.19
  334.7 14.5 %add_convert_fusion = bf16[32,8,64,128]{3,2,1,0:T(8,128)(2,1)S(1)} fusion(bf16[32,8,64,128]{3,2,1,0:T(8,128)(2,1)S(1)} %bitcast.97, f32[32,8]{1,0:T(8,128)S(1)} %copy-done.17, f32[32,32,8,64]{3,2,1,0:T(8,128)S(1)} %copy-done.3, f32[32,32,256]{2,1,0:T(8,128)S(1)} %copy-done.4), kind=kOutput, calls=%fused_computation.4 | convolution fusion | flops 813694976 | bytes 13123584 | tf_op jit(solution)/shard_map/sht,sthp,stn->shpn/dot_general | solution.py:101
  349.2 6.1 convolution_convert_fusion
  355.3 10.6 %all_to_all.61 = bf16[32,2,65536]{2,1,0:T(2,128)(2,1)} reshape(bf16[64,65536]{1,0:T(8,128)(2,1)} %convolution_convert_fusion) | data formatting | bytes 16777216 | tf_op jit(solution)/shard_map/all_to_all | solution.py:234
  365.9 10.0 %all-to-all-start.4 = ((bf16[32,2,65536]{2,1,0:T(2,128)(2,1)}), bf16[32,2,65536]{2,1,0:T(2,128)(2,1)}, u32[]{:S(2)}, u32[]{:S(2)}) async-start(bf16[32,2,65536]{2,1,0:T(2,128)(2,1)} %all_to_all.61), calls=%async_computation.4 | async-start | bytes 16777216 | tf_op jit(solution)/shard_map/all_to_all | solution.py:234
  384.7 3.7 broadcast_multiply_fusion.1
  388.4 8.9 %fusion.54 = f32[8,128,8,64]{1,3,2,0:T(8,128)S(1)} fusion(f32[8,128,128]{2,1,0:T(8,128)S(1)} %copy-done.14, f32[8,8,128]{2,1,0:T(8,128)S(1)} %copy.96, pred[128,128]{1,0:T(8,128)(4,1)S(1)} %fusion.80, f32[8,128,8,64]{3,2,1,0:T(8,128)S(1)} %broadcast_multiply_fusion.1), kind=kOutput, calls=%fused_computation.77 | convolution fusion | flops 809500672 | bytes 4767744 | tf_op jit(solution)/shard_map/bhtu,buhp->bthp/dot_general | solution.py:90
  403.0 4.6 fusion.51
  407.6 109.3 %all-gather.2.cloned.1.call-done = bf16[32,64,512]{2,1,0:T(8,128)(2,1)} async-done(((bf16[1,64,512]{2,1,0:T(8,128)(2,1)}), bf16[32,64,512]{2,1,0:T(8,128)(2,1)}) %all-gather.2.cloned.1.call-update) | async-done | bytes 2097168 | tf_op jit(solution)/shard_map/all_gather | solution.py:264
  516.8 4.8 fusion.48
  521.7 13.9 %fusion.7 = f32[32,32,8,64]{3,1,2,0:T(8,128)S(1)} fusion(f32[32,32,8,64]{3,2,1,0:T(8,128)S(1)} %copy-done, f32[32,32,8,64]{3,2,1,0:T(8,128)} %bitcast.100, bf16[32,8,64,128]{3,2,1,0:T(8,128)(2,1)} %bitcast.98, f32[32,32]{1,0:T(8,128)S(1)} %fusion.105, f32[8]{0:T(128)S(1)} %copy-done.36, f32[32,32,8]{1,2,0:T(8,128)S(1)} %bitcast_exponential_fusion.1, ...), kind=kOutput, calls=%fused_computation.17 | convolution fusion | flops 807927808 | bytes 13255168 | tf_op jit(solution)/shard_map/stn,shpn->sthp/dot_general | solution.py:93
  535.6 5.8 copy.103
  541.4 3.5 reshape.251
  545.7 27.4 %psum.14 = f32[32,32]{1,0:T(8,128)S(1)} all-reduce(f32[32,32]{1,0:T(8,128)S(1)} %multiply_reduce_fusion), channel_id=1, replica_groups=mesh['section'=8,'row'=32] {'section'}, use_global_device_ids=true, to_apply=%region_6.7 | all-reduce | flops 1024 | bytes 8192 | tf_op jit(solution)/shard_map/psum | solution.py:260
  576.1 29.2 %all-reduce.1 = bf16[32,32,64]{2,1,0:T(8,128)(2,1)S(1)} all-reduce(f32[32,32,64]{2,1,0:T(8,128)S(1)} %fusion.39), channel_id=1, replica_groups=mesh['section'=8,'row'=32] {'section'}, use_global_device_ids=true, to_apply=%region_7.8 | all-reduce | flops 65536 | bytes 393216 | tf_op jit(solution)/shard_map/psum | solution.py:279
  605.3 3.6 fusion.59
  608.9 10.3 %all_to_all.63 = bf16[64,65536]{1,0:T(8,128)(2,1)} reshape(bf16[32,2,65536]{2,1,0:T(2,128)(2,1)} %all-to-all-done.4) | data formatting | bytes 16777216 | tf_op jit(solution)/shard_map/all_to_all | solution.py:234
  619.2 4.7 fusion.20
  (159 shorter events, 63.9 us)
Async XLA Ops:
  10.5 30.0 %copy-start.28 = (s32[64]{0:T(128)}, s32[64]{0:T(128)S(1)}, u32[]{:S(2)}) copy-start(s32[64]{0:T(128)S(1)} %select_reduce_fusion.3) | copy-start | bytes 772
  11.0 29.5 %copy-start.29 = (pred[64]{0:T(512)(128)(4,1)}, pred[64]{0:T(512)(128)(4,1)S(1)}, u32[]{:S(2)}) copy-start(pred[64]{0:T(512)(128)(4,1)S(1)} %fusion.98) | copy-start | bytes 196
  12.7 20.2 %all-to-all-start.1 = ((bf16[32,2,768]{2,1,0:T(2,128)(2,1)}), bf16[32,2,768]{2,1,0:T(2,128)(2,1)S(1)}, u32[]{:S(2)}, u32[]{:S(2)}) async-start(bf16[32,2,768]{2,1,0:T(2,128)(2,1)} %all_to_all.54), calls=%async_computation.1 | async-start | bytes 196608 | tf_op jit(solution)/shard_map/all_to_all | solution.py:212
  24.4 32.6 %copy-start.26 = (s32[32]{0:T(128)}, s32[32]{0:T(128)S(1)}, u32[]{:S(2)}) copy-start(s32[32]{0:T(128)S(1)} %dynamic_slice.9) | copy-start | bytes 388
  24.5 25.0 %copy-start.22 = (s32[64]{0:T(128)}, s32[64]{0:T(128)S(1)}, u32[]{:S(2)}) copy-start(s32[64]{0:T(128)S(1)} %select_reduce_fusion.2) | copy-start | bytes 772
  24.5 24.9 %copy-start.24 = (pred[64]{0:T(512)(128)(4,1)}, pred[64]{0:T(512)(128)(4,1)S(1)}, u32[]{:S(2)}) copy-start(pred[64]{0:T(512)(128)(4,1)S(1)} %fusion.94) | copy-start | bytes 196
  26.1 35.0 %copy-start.2 = (f32[32,32,512]{2,1,0:T(8,128)}, f32[32,32,512]{2,1,0:T(8,128)S(1)}, u32[]{:S(2)}) copy-start(f32[32,32,512]{2,1,0:T(8,128)S(1)} %convert_element_type.117) | copy-start | bytes 6291460
  30.0 27.0 %copy-start.33 = (s32[32]{0:T(128)}, s32[32]{0:T(128)S(1)}, u32[]{:S(2)}) copy-start(s32[32]{0:T(128)S(1)} %dynamic_slice.10) | copy-start | bytes 388
  32.9 16.5 %all-to-all-start = ((bf16[32,2,1536]{2,1,0:T(2,128)(2,1)}), bf16[32,2,1536]{2,1,0:T(2,128)(2,1)S(1)}, u32[]{:S(2)}, u32[]{:S(2)}) async-start(bf16[32,2,1536]{2,1,0:T(2,128)(2,1)} %all_to_all.51), calls=%async_computation | async-start | bytes 393216 | tf_op jit(solution)/shard_map/all_to_all | solution.py:205
  43.2 37.6 %copy-start.10 = (f32[32,3,256]{2,1,0:T(4,128)}, f32[32,3,256]{2,1,0:T(4,128)S(1)}, u32[]{:S(2)}) copy-start(f32[32,3,256]{2,1,0:T(4,128)S(1)} %reshape.260) | copy-start | bytes 294916
  49.4 15.5 %all-to-all-start.6 = ((bf16[32,2,768]{2,1,0:T(2,128)(2,1)}), bf16[32,2,768]{2,1,0:T(2,128)(2,1)}, u32[]{:S(2)}, u32[]{:S(2)}) async-start(bf16[32,2,768]{2,1,0:T(2,128)(2,1)} %all_to_all.67), calls=%async_computation.6 | async-start | bytes 196608 | tf_op jit(solution)/shard_map/all_to_all | solution.py:248
  64.9 26.5 %all-to-all-start.5 = ((bf16[32,2,1536]{2,1,0:T(2,128)(2,1)}), bf16[32,2,1536]{2,1,0:T(2,128)(2,1)S(1)}, u32[]{:S(2)}, u32[]{:S(2)}) async-start(bf16[32,2,1536]{2,1,0:T(2,128)(2,1)} %all_to_all.64), calls=%async_computation.5 | async-start | bytes 393216 | tf_op jit(solution)/shard_map/all_to_all | solution.py:241
  91.4 10.5 %copy-start.37 = (f32[8]{0:T(128)S(1)}, f32[8]{0:T(128)}, u32[]{:S(2)}) copy-start(f32[8]{0:T(128)} %param.29) | copy-start | bytes 100
  91.4 10.6 %copy-start.34 = (s32[32]{0:T(128)S(1)}, s32[32]{0:T(128)}, u32[]{:S(2)}) copy-start(s32[32]{0:T(128)} %copy-done.33) | copy-start | bytes 388
  91.4 190.9 %copy-start.18 = (bf16[1,64,512]{2,1,0:T(8,128)(2,1)S(1)}, bf16[1,64,512]{2,1,0:T(8,128)(2,1)}, u32[]{:S(2)}) copy-start(bf16[1,64,512]{2,1,0:T(8,128)(2,1)} %param.36) | copy-start | bytes 196612
  92.1 190.2 %all-to-all-start.2 = ((bf16[32,2,65536]{2,1,0:T(2,128)(2,1)}), bf16[32,2,65536]{2,1,0:T(2,128)(2,1)}, u32[]{:S(2)}, u32[]{:S(2)}) async-start(bf16[32,2,65536]{2,1,0:T(2,128)(2,1)} %all_to_all.57), calls=%async_computation.2 | async-start | bytes 16777216 | tf_op jit(solution)/shard_map/all_to_all | solution.py:198
  101.9 191.8 %copy-start.16 = (bf16[32,8,32]{2,1,0:T(8,128)(2,1)S(1)}, bf16[32,8,32]{2,1,0:T(8,128)(2,1)}, u32[]{:S(2)}) copy-start(bf16[32,8,32]{2,1,0:T(8,128)(2,1)} %param.23) | copy-start | bytes 49156
  102.0 191.8 %copy-start.32 = (f32[8]{0:T(128)S(1)}, f32[8]{0:T(128)}, u32[]{:S(2)}) copy-start(f32[8]{0:T(128)} %param.28) | copy-start | bytes 100
  282.3 20.5 %copy-start.30 = (f32[4,256]{1,0:T(4,128)S(1)}, f32[4,256]{1,0:T(4,128)}, u32[]{:S(2)}) copy-start(f32[4,256]{1,0:T(4,128)} %param.25) | copy-start | bytes 12292
  282.3 20.5 %copy-start.21 = (f32[4,512]{1,0:T(4,128)S(1)}, f32[4,512]{1,0:T(4,128)}, u32[]{:S(2)}) copy-start(f32[4,512]{1,0:T(4,128)} %param.24) | copy-start | bytes 24580
  282.3 20.6 %copy-start.11 = (f32[32,3,256]{2,1,0:T(4,128)S(1)}, f32[32,3,256]{2,1,0:T(4,128)}, u32[]{:S(2)}) copy-start(f32[32,3,256]{2,1,0:T(4,128)} %copy-done.10) | copy-start | bytes 294916
  282.4 20.6 %copy-start.35 = (f32[256]{0:T(256)S(1)}, f32[256]{0:T(256)}, u32[]{:S(2)}) copy-start(f32[256]{0:T(256)} %param.27) | copy-start | bytes 3076
  284.0 82.0 %all-to-all-start.3 = ((bf16[32,1,64,512]{3,2,1,0:T(8,128)(2,1)}), bf16[32,1,64,512]{3,2,1,0:T(8,128)(2,1)}, u32[]{:S(2)}, u32[]{:S(2)}) async-start(bf16[32,1,64,512]{3,2,1,0:T(8,128)(2,1)} %stack.2), calls=%async_computation.3 | async-start | bytes 4194304 | tf_op jit(solution)/shard_map/all_to_all | solution.py:155
  331.9 17.3 %copy-start.1 = (bf16[4,8,512,128]{3,2,1,0:T(8,128)(2,1)}, bf16[4,8,512,128]{3,2,1,0:T(8,128)(2,1)S(1)}, u32[]{:S(2)}) copy-start(bf16[4,8,512,128]{3,2,1,0:T(8,128)(2,1)S(1)} %copy.125) | copy-start | bytes 12582916
  334.7 14.5 %copy-start.23 = (s32[64]{0:T(128)S(1)}, s32[64]{0:T(128)}, u32[]{:S(2)}) copy-start(s32[64]{0:T(128)} %copy-done.22) | copy-start | bytes 772
  334.7 14.5 %copy-start.25 = (pred[64]{0:T(512)(128)(4,1)S(1)}, pred[64]{0:T(512)(128)(4,1)}, u32[]{:S(2)}) copy-start(pred[64]{0:T(512)(128)(4,1)} %copy-done.24) | copy-start | bytes 196
  365.9 12.2 %copy-start.15 = (f32[32,32,8]{1,2,0:T(8,128)S(1)}, f32[32,32,8]{1,2,0:T(8,128)}, u32[]{:S(2)}) copy-start(f32[32,32,8]{1,2,0:T(8,128)} %get-tuple-element.33) | copy-start | bytes 98308
  365.9 242.9 %all-to-all-start.4 = ((bf16[32,2,65536]{2,1,0:T(2,128)(2,1)}), bf16[32,2,65536]{2,1,0:T(2,128)(2,1)}, u32[]{:S(2)}, u32[]{:S(2)}) async-start(bf16[32,2,65536]{2,1,0:T(2,128)(2,1)} %all_to_all.61), calls=%async_computation.4 | async-start | bytes 16777216 | tf_op jit(solution)/shard_map/all_to_all | solution.py:234
  375.9 140.9 %all-gather.2.cloned.1.call-start = ((), (), s32[]{:S(2)}) async-start(), calls=%async_computation.7 | async-start | bytes 2162688 | tf_op jit(solution)/shard_map/all_gather | solution.py:264
  403.0 118.7 %copy-start.36 = (f32[8]{0:T(128)S(1)}, f32[8]{0:T(128)}, u32[]{:S(2)}) copy-start(f32[8]{0:T(128)} %param.30) | copy-start | bytes 100
  541.4 31.7 %copy-start.31 = (f32[512]{0:T(512)S(1)}, f32[512]{0:T(512)}, u32[]{:S(2)}) copy-start(f32[512]{0:T(512)} %param.31) | copy-start | bytes 6148
  574.8 30.4 %copy-start.6 = (bf16[32,64,512]{2,0,1:T(8,128)(2,1)S(1)}, bf16[32,64,512]{2,0,1:T(8,128)(2,1)}, u32[]{:S(2)}) copy-start(bf16[32,64,512]{2,0,1:T(8,128)(2,1)} %fusion.51) | copy-start | bytes 6291460
  (14 other events, 47.9 us)
Sparse Core Ops, SparseCore 0:
  379.3 137.4 all-gather.1
